TPU v7x, 512 devices: a whole 4x8x8 slice. The times are simulated.
512 devices in a mesh: ep: 64 (over z, y), tp: 8 (over x, core).
Axes of the slice: x: 4, y: 8, z: 8, core: 2. Of those that a mesh axis runs over, the one named last changes fastest.
Arguments:
- patches: bfloat16 [32768, 1024], P('ep', 'tp'), may hold values from -6 to 6
- patch_grad: bfloat16 [32768, 1024], P('ep', 'tp'), may hold values from -1.796875 to 1.796875
- expert_up: bfloat16 [64, 1024, 4096], P('ep', None, 'tp'), may hold values from -0.1875 to 0.1875
- expert_down: bfloat16 [64, 4096, 1024], P('ep', 'tp'), may hold values from -0.09375 to 0.09375
- expert_counts: int32 [64, 64], P('ep'), may hold values from 1 to 16, as said below
Outputs:
- input_grad: bfloat16 [32768, 1024], P('ep', 'tp')
- up_grad: bfloat16 [64, 1024, 4096], P('ep', None, 'tp')
- down_grad: bfloat16 [64, 4096, 1024], P('ep', 'tp')
Inputs may be any that keep to these rules, and one draw needn't show every extreme that they name: `expert_counts`: row s gives, for each of the 64 experts in order, how many of the 512 rows of ep index s are routed to it; those rows stand together in expert order. Every row sums to 512, and one expert has exactly 16 rows from every index of ep.
All inputs are finite; a program needn't handle non-finite values.
Results may differ from a plain program's by a relative error of at most 0.0049.
Values may be sent and summed in bfloat16 or wider, within the bound.
No kernel may reach another device: no remote copies, remote signals or barrier semaphores. Data moves between devices by JAX's collectives and lax.ppermute only.
A program may use at most 64 MiB of HBM per device.

v0:
```python
import jax
import jax.numpy as jnp
from jax import lax
from jax.sharding import PartitionSpec as P


def activation(values):
    return jax.nn.gelu(values, approximate=True)


def slot_plan(counts_row, row_count, capacity):
    experts = counts_row.shape[0]
    row_ends = jnp.cumsum(counts_row)
    row_starts = row_ends - counts_row
    positions = lax.broadcasted_iota(jnp.int32, (experts, capacity), 1)
    slot_live = positions < counts_row[:, None]
    slot_source = jnp.where(slot_live, row_starts[:, None] + positions, 0)
    row_ids = lax.broadcasted_iota(jnp.int32, (row_count, experts), 0)
    row_expert = jnp.sum((row_ids >= row_ends[None, :]).astype(jnp.int32), axis=1)
    expert_ids = lax.broadcasted_iota(jnp.int32, (row_count, experts), 1)
    own_start = jnp.sum(
        jnp.where(row_expert[:, None] == expert_ids, row_starts[None, :], 0), axis=1
    )
    row_numbers = lax.broadcasted_iota(jnp.int32, (row_count,), 0)
    row_slot = row_expert * capacity + row_numbers - own_start
    return (slot_live, slot_source, row_slot)


def fill_slots(source_table, slot_live, slot_source):
    picked = jnp.take(source_table, slot_source.reshape(-1), axis=0)
    picked = picked.reshape(slot_source.shape + (source_table.shape[1],))
    return jnp.where(slot_live[:, :, None], picked, jnp.zeros((), source_table.dtype))


def per_device(patches, patch_grad, expert_up, expert_down, expert_counts):
    row_count = patches.shape[0]
    experts = expert_counts.shape[1]
    capacity = 2 * row_count // experts
    slot_live, slot_source, row_slot = slot_plan(expert_counts[0], row_count, capacity)
    weight_up = expert_up[0]
    weight_down = expert_down[0]
    gathered_rows, gathered_grads = (
        lax.all_gather(patches, "tp", axis=1, tiled=True),
        lax.all_gather(patch_grad, "tp", axis=1, tiled=True),
    )
    send_rows = fill_slots(gathered_rows, slot_live, slot_source)
    send_grads = fill_slots(gathered_grads, slot_live, slot_source)
    got_rows, got_grads = (
        lax.all_to_all(send_rows, "ep", split_axis=0, concat_axis=0, tiled=True),
        lax.all_to_all(send_grads, "ep", split_axis=0, concat_axis=0, tiled=True),
    )
    sources = got_rows.shape[0]
    feature_width = got_rows.shape[2]
    slot_rows = got_rows.reshape(sources * capacity, feature_width)
    slot_grads = got_grads.reshape(sources * capacity, feature_width)
    pre_act = jnp.dot(slot_rows, weight_up, preferred_element_type=jnp.float32)
    act_value, act_back = jax.vjp(activation, pre_act)
    hidden = act_value.astype(jnp.bfloat16)
    hidden_grad = lax.dot_general(
        slot_grads, weight_down, (((1,), (1,)), ((), ())), preferred_element_type=jnp.float32
    )
    pre_grad = act_back(hidden_grad)[0].astype(jnp.bfloat16)
    down_part = lax.dot_general(
        hidden, slot_grads, (((0,), (0,)), ((), ())), preferred_element_type=jnp.float32
    )
    up_part = lax.dot_general(
        slot_rows, pre_grad, (((0,), (0,)), ((), ())), preferred_element_type=jnp.float32
    )
    row_term = lax.dot_general(
        pre_grad, weight_up, (((1,), (1,)), ((), ())), preferred_element_type=jnp.float32
    )
    summed = lax.psum_scatter(row_term, "tp", scatter_dimension=1, tiled=True)
    back_rows = summed.astype(jnp.bfloat16).reshape(sources, capacity, summed.shape[1])
    returned = lax.all_to_all(back_rows, "ep", split_axis=0, concat_axis=0, tiled=True)
    input_grad = jnp.take(returned.reshape(experts * capacity, returned.shape[2]), row_slot, axis=0)
    return (input_grad, up_part.astype(jnp.bfloat16)[None], down_part.astype(jnp.bfloat16)[None])


def solution(mesh):
    return jax.shard_map(
        per_device,
        mesh=mesh,
        in_specs=(
            P("ep", "tp"),
            P("ep", "tp"),
            P("ep", None, "tp"),
            P("ep", "tp", None),
            P("ep", None),
        ),
        out_specs=(P("ep", "tp"), P("ep", None, "tp"), P("ep", "tp", None)),
        check_vma=False,
    )
```

profile of v0, /device:TPU:8, one launch (start us, length us, event | category | flops | bytes accessed | tf_op | source)
XLA Modules:
  0.0 298.1 jit_solution(2394442050553680179)
XLA Ops:
  7.2 0.0 copy-start
  7.2 0.0 all-gather.3.cloned.1.call-start
  7.2 0.7 all-gather.3.cloned.1.call-update
  7.9 0.0 all-gather.5.cloned.1.call-start
  8.0 0.7 all-gather.5.cloned.1.call-update
  8.7 0.7 copy.10
  9.4 0.1 reduce-window.4
  9.5 0.1 reduce
  9.6 0.7 bitcast_subtract_fusion.1
  10.3 0.7 add_select_fusion
  11.0 0.1 select_n.49
  11.1 0.7 iota_compare_fusion.2
  11.9 31.4 %all-gather.3.cloned.1.call-done = bf16[512,1024]{1,0:T(8,128)(2,1)} async-done(((bf16[512,128]{1,0:T(8,128)(2,1)}), bf16[512,1024]{1,0:T(8,128)(2,1)}) %all-gather.3.cloned.1.call-update) | async-done | bytes 1048592 | tf_op jit(solution)/shard_map/all_gather | solution.py:44
  43.3 6.3 %gather_fusion.1 = bf16[1024,1024]{1,0:T(8,128)(2,1)S(1)} fusion(bf16[512,1024]{1,0:T(8,128)(2,1)} %all-gather.3.cloned.1.call-done, s32[1024]{0:T(1024)S(1)} %fusion.21), kind=kCustom, calls=%fused_computation.clone | custom fusion | bytes 4198400 | tf_op jit(solution)/shard_map/jit(_take)/gather | solution.py:30
  49.6 25.4 %all-gather.5.cloned.1.call-done = bf16[512,1024]{1,0:T(8,128)(2,1)} async-done(((bf16[512,128]{1,0:T(8,128)(2,1)}), bf16[512,1024]{1,0:T(8,128)(2,1)}) %all-gather.5.cloned.1.call-update) | async-done | bytes 1048592 | tf_op jit(solution)/shard_map/all_gather | solution.py:43
  75.0 7.4 %gather_fusion.2 = bf16[1024,1024]{1,0:T(8,128)(2,1)} fusion(bf16[512,1024]{1,0:T(8,128)(2,1)} %all-gather.5.cloned.1.call-done, s32[1024]{0:T(1024)S(1)} %fusion.21), kind=kCustom, calls=%fused_computation.1.clone | custom fusion | bytes 4198400 | tf_op jit(solution)/shard_map/jit(_take)/gather | solution.py:30
  82.4 2.0 broadcast_select_fusion.1
  84.5 1.7 broadcast_select_fusion.3
  86.2 66.0 %all_to_all.15 = bf16[64,16,1024]{2,1,0:T(8,128)(2,1)S(1)} all-to-all(bf16[64,16,1024]{2,1,0:T(8,128)(2,1)S(1)} %get-tuple-element.5), channel_id=1, replica_groups=mesh['ep'=64,'tp'=8] {'ep'}, dimensions={0} | all-to-all | bytes 4194304 | tf_op jit(solution)/shard_map/all_to_all | solution.py:49
  152.2 8.6 %all-to-all-start = ((bf16[64,16,1024]{2,1,0:T(8,128)(2,1)}), bf16[64,16,1024]{2,1,0:T(8,128)(2,1)}, u32[]{:S(2)}, u32[]{:S(2)}) async-start(bf16[64,16,1024]{2,1,0:T(8,128)(2,1)} %get-tuple-element.4), calls=%async_computation | async-start | bytes 4194304 | tf_op jit(solution)/shard_map/all_to_all | solution.py:50
  160.8 0.0 reduce-scatter.2.cloned.1.call-start
  160.8 0.0 copy-done
  160.8 2.6 fusion.11
  163.4 49.6 %all-to-all-done = bf16[64,16,1024]{2,1,0:T(8,128)(2,1)} async-done(((bf16[64,16,1024]{2,1,0:T(8,128)(2,1)}), bf16[64,16,1024]{2,1,0:T(8,128)(2,1)}, u32[]{:S(2)}, u32[]{:S(2)}) %all-to-all-start) | async-done | bytes 2097184 | tf_op jit(solution)/shard_map/all_to_all | solution.py:50
  213.0 4.9 %fusion.6 = bf16[1024,512]{1,0:T(8,128)(2,1)S(1)} fusion(f32[1024,512]{1,0:T(8,128)} %fusion.11, bf16[1024,1024]{1,0:T(8,128)(2,1)} %bitcast.4, bf16[1,512,1024]{2,1,0:T(8,128)(2,1)} %param.10), kind=kOutput, calls=%fused_computation.11 | convolution fusion | flops 1084227584 | bytes 6291456 | tf_op jit(solution)/shard_map/dot_general | solution.py:59
  217.9 0.0 copy-start.2
  217.9 1.0 copy-done.2
  218.9 3.2 %fusion.9 = f32[1024,1024]{1,0:T(8,128)} fusion(bf16[1024,512]{1,0:T(8,128)(2,1)S(1)} %fusion.6, bf16[1,1024,512]{2,1,0:T(8,128)(2,1)S(1)} %copy-done), kind=kOutput, calls=%fused_computation.21 | convolution fusion | flops 1073741824 | bytes 6291456 | tf_op jit(solution)/shard_map/dot_general | solution.py:69
  222.1 0.0 copy-start.1
  222.1 0.0 reduce-scatter.2.cloned.1.call-update
  222.1 0.1 convert_reduce_fusion
  222.2 0.5 copy-done.1
  222.8 0.1 select_reduce_fusion
  222.9 38.3 %reduce-scatter.2.cloned.1.call-done = f32[1024,128]{1,0:T(8,128)} async-done(((f32[1024,1024]{1,0:T(8,128)}), f32[1024,128]{1,0:T(8,128)}) %reduce-scatter.2.cloned.1.call-update) | async-done | bytes 524304 | tf_op jit(solution)/shard_map/reduce_scatter | solution.py:72
  261.2 1.8 convert_element_type.20
  263.0 13.4 %all-to-all-start.2 = ((bf16[64,16,128]{2,1,0:T(8,128)(2,1)}), bf16[64,16,128]{2,1,0:T(8,128)(2,1)S(1)}, u32[]{:S(2)}, u32[]{:S(2)}) async-start(bf16[64,16,128]{2,1,0:T(8,128)(2,1)} %bitcast.43), calls=%async_computation.3 | async-start | bytes 524288 | tf_op jit(solution)/shard_map/all_to_all | solution.py:74
  276.4 0.0 copy-start.3
  276.4 3.6 %fusion.7 = bf16[1,1024,512]{2,1,0:T(8,128)(2,1)} fusion(bf16[1024,1024]{1,0:T(8,128)(2,1)S(1)} %bitcast.42, bf16[1024,512]{1,0:T(8,128)(2,1)} %copy-done.2), kind=kOutput, calls=%fused_computation.19 | convolution fusion | flops 1074266112 | bytes 4194304 | tf_op jit(solution)/shard_map/dot_general | solution.py:66
  280.0 0.0 copy-done.3
  280.0 4.0 %fusion.8 = bf16[1,512,1024]{2,1,0:T(8,128)(2,1)} fusion(bf16[1024,1024]{1,0:T(8,128)(2,1)} %bitcast.4, f32[1024,512]{1,0:T(8,128)S(1)} %copy-done.3), kind=kOutput, calls=%fused_computation.20 | convolution fusion | flops 1078984704 | bytes 5242880 | tf_op jit(solution)/shard_map/dot_general | solution.py:63
  284.0 5.4 %all-to-all-done.2 = bf16[64,16,128]{2,1,0:T(8,128)(2,1)S(1)} async-done(((bf16[64,16,128]{2,1,0:T(8,128)(2,1)}), bf16[64,16,128]{2,1,0:T(8,128)(2,1)S(1)}, u32[]{:S(2)}, u32[]{:S(2)}) %all-to-all-start.2) | async-done | bytes 262176 | tf_op jit(solution)/shard_map/all_to_all | solution.py:74
  289.4 1.3 gather_fusion
  290.8 0.8 broadcast_select_fusion.4
  (7 shorter events, 0.0 us)
Async XLA Ops:
  7.2 153.7 %copy-start = (bf16[1,1024,512]{2,1,0:T(8,128)(2,1)S(1)}, bf16[1,1024,512]{2,1,0:T(8,128)(2,1)}, u32[]{:S(2)}) copy-start(bf16[1,1024,512]{2,1,0:T(8,128)(2,1)} %param.9) | copy-start | bytes 3145732
  7.2 36.1 %all-gather.3.cloned.1.call-start = ((), (), s32[]{:S(2)}) async-start(), calls=%async_computation.4 | async-start | bytes 1179648 | tf_op jit(solution)/shard_map/all_gather | solution.py:44
  7.9 67.1 %all-gather.5.cloned.1.call-start = ((), (), s32[]{:S(2)}) async-start(), calls=%async_computation.5 | async-start | bytes 1179648 | tf_op jit(solution)/shard_map/all_gather | solution.py:43
  152.2 60.8 %all-to-all-start = ((bf16[64,16,1024]{2,1,0:T(8,128)(2,1)}), bf16[64,16,1024]{2,1,0:T(8,128)(2,1)}, u32[]{:S(2)}, u32[]{:S(2)}) async-start(bf16[64,16,1024]{2,1,0:T(8,128)(2,1)} %get-tuple-element.4), calls=%async_computation | async-start | bytes 4194304 | tf_op jit(solution)/shard_map/all_to_all | solution.py:50
  160.8 100.5 %reduce-scatter.2.cloned.1.call-start = ((), (), s32[]{:S(2)}) async-start(), calls=%async_computation.6 | async-start | bytes 4718592 | tf_op jit(solution)/shard_map/reduce_scatter | solution.py:72
  217.9 1.0 copy-start.2
  222.1 0.7 copy-start.1
  263.0 26.4 %all-to-all-start.2 = ((bf16[64,16,128]{2,1,0:T(8,128)(2,1)}), bf16[64,16,128]{2,1,0:T(8,128)(2,1)S(1)}, u32[]{:S(2)}, u32[]{:S(2)}) async-start(bf16[64,16,128]{2,1,0:T(8,128)(2,1)} %bitcast.43), calls=%async_computation.3 | async-start | bytes 524288 | tf_op jit(solution)/shard_map/all_to_all | solution.py:74
  276.4 3.6 %copy-start.3 = (f32[1024,512]{1,0:T(8,128)S(1)}, f32[1024,512]{1,0:T(8,128)}, u32[]{:S(2)}) copy-start(f32[1024,512]{1,0:T(8,128)} %fusion.11) | copy-start | bytes 6291460
Sparse Core Ops, SparseCore 0:
  10.1 33.1 all-gather.2
  45.4 29.5 all-gather.4
  222.3 38.9 reduce-scatter.1
where the time goes:
time: 299 us; the launch traced here: 298 us
  waiting for transfers between devices  152 us (51%)
  blocking collectives  66 us (22%)
  starting transfers between devices  22.1 us (7%)
  matrix products  18.3 us (6%)
  local copies, waits for them, and re-layouts  17.4 us (6%)
  between operations  13.9 us (5%)
  other arithmetic  8.85 us (3%)
    all_to_all x1, blocking collectives, per_device(): lax.all_to_all(send_rows, 'ep', split_axis=0, concat_axis=0, tiled=True)  66 us
    all_to_all x1, waiting for transfers between devices, per_device(): lax.all_to_all(send_grads, 'ep', split_axis=0, concat_axis=0, tiled=True)  49.6 us
    reduce_scatter x1, waiting for transfers between devices, per_device(): summed = lax.psum_scatter(row_term, 'tp', scatter_dimension=1, tiled=True)  38.3 us
    all_gather x1, waiting for transfers between devices, per_device(): lax.all_gather(patch_grad, 'tp', axis=1, tiled=True)  31.4 us
    all_gather x1, waiting for transfers between devices, per_device(): lax.all_gather(patches, 'tp', axis=1, tiled=True)  25.4 us
    gather x2, local copies, waits for them, and re-layouts, fill_slots(): picked = jnp.take(source_table, slot_source.reshape(-1), axis=0)  13.7 us
    all_to_all x1, starting transfers between devices, per_device(): lax.all_to_all(back_rows, 'ep', split_axis=0, concat_axis=0, tiled=True)  13.4 us
    all_to_all x1, starting transfers between devices, per_device(): lax.all_to_all(send_grads, 'ep', split_axis=0, concat_axis=0, tiled=True)  8.57 us
  transfers between devices with their start and end apart: 5, of which 5 were waited for; matrix products, arithmetic and copies ran while one was open for 7% of the time, Pallas kernels for 0%

commit v1 on v0

--- a/solution.py
+++ b/solution.py
@@ -40,7 +40,9 @@
     weight_up = expert_up[0]
     weight_down = expert_down[0]
     gathered_rows, gathered_grads = (
-        lax.all_gather(patches, "tp", axis=1, tiled=True),
+        jnp.concatenate(
+            lax.all_to_all(jnp.stack([patches] * lax.axis_size("tp")), "tp", 0, 0), axis=1
+        ),
         lax.all_gather(patch_grad, "tp", axis=1, tiled=True),
     )
     send_rows = fill_slots(gathered_rows, slot_live, slot_source)

time: 299 us -> 267 us (0.89)
  waiting for transfers between devices: 152 us -> 117 us
  starting transfers between devices: 22.1 us -> 26.3 us
    all_gather x1 -> x0, waiting for transfers between devices: 25.4 us -> none  [per_device(): lax.all_gather(patches, 'tp', axis=1, tiled=True)]
    all_gather x1, waiting for transfers between devices: 31.4 us -> 7.62 us  [per_device(): lax.all_gather(patch_grad, 'tp', axis=1, tiled=True)]
    all_to_all x0 -> x1, waiting for transfers between devices: none -> 15.3 us  [per_device(): lax.all_to_all(jnp.stack([patches] * lax.axis_size('tp')), 'tp', 0, 0)]
    all_to_all x0 -> x1, starting transfers between devices: none -> 4.3 us  [per_device(): lax.all_to_all(jnp.stack([patches] * lax.axis_size('tp')), 'tp', 0, 0)]
where the time goes in v1:
time: 267 us
  waiting for transfers between devices  117 us (44%)
  blocking collectives  66.2 us (25%)
  starting transfers between devices  26.3 us (10%)
  matrix products  18.3 us (7%)
  local copies, waits for them, and re-layouts  17.4 us (7%)
  between operations  14.2 us (5%)
  other arithmetic  6.88 us (3%)
    all_to_all x1, blocking collectives, per_device(): lax.all_to_all(send_rows, 'ep', split_axis=0, concat_axis=0, tiled=True)  66.2 us
    all_to_all x1, waiting for transfers between devices, per_device(): lax.all_to_all(send_grads, 'ep', split_axis=0, concat_axis=0, tiled=True)  49.5 us
    reduce_scatter x1, waiting for transfers between devices, per_device(): summed = lax.psum_scatter(row_term, 'tp', scatter_dimension=1, tiled=True)  38.8 us
    all_to_all x1, waiting for transfers between devices, per_device(): lax.all_to_all(jnp.stack([patches] * lax.axis_size('tp')), 'tp', 0, 0)  15.3 us
    all_to_all x1, starting transfers between devices, per_device(): lax.all_to_all(back_rows, 'ep', split_axis=0, concat_axis=0, tiled=True)  13.4 us
    gather x2, local copies, waits for them, and re-layouts, fill_slots(): picked = jnp.take(source_table, slot_source.reshape(-1), axis=0)  12.7 us
    all_to_all x1, starting transfers between devices, per_device(): lax.all_to_all(send_grads, 'ep', split_axis=0, concat_axis=0, tiled=True)  8.57 us
    all_gather x1, waiting for transfers between devices, per_device(): lax.all_gather(patch_grad, 'tp', axis=1, tiled=True)  7.62 us
  transfers between devices with their start and end apart: 5, of which 5 were waited for; matrix products, arithmetic and copies ran while one was open for 7% of the time, Pallas kernels for 0%

profile of v1, /device:TPU:8, one launch (start us, length us, event | category | flops | bytes accessed | tf_op | source)
XLA Modules:
  0.0 266.8 jit_solution(1678048613685465293)
XLA Ops:
  7.2 0.0 copy-start
  7.2 0.0 copy-start.2
  7.2 0.0 all-gather.2.cloned.1.call-start
  7.2 0.7 all-gather.2.cloned.1.call-update
  7.9 2.0 stack.2
  9.9 4.3 %all-to-all-start.1 = ((bf16[8,512,128]{2,1,0:T(8,128)(2,1)}), bf16[8,512,128]{2,1,0:T(8,128)(2,1)S(1)}, u32[]{:S(2)}, u32[]{:S(2)}) async-start(bf16[8,512,128]{2,1,0:T(8,128)(2,1)} %stack.2), calls=%async_computation.1 | async-start | bytes 2097152 | tf_op jit(solution)/shard_map/all_to_all | solution.py:44
  14.2 0.0 copy-done.2
  14.2 0.1 copy.12
  14.3 0.1 reduce-window.4
  14.4 0.1 reduce
  14.6 0.1 add_select_fusion
  14.7 0.1 select_n.49
  14.8 0.1 iota_compare_fusion.2
  14.8 15.3 %all-to-all-done.1 = bf16[8,512,128]{2,1,0:T(8,128)(2,1)S(1)} async-done(((bf16[8,512,128]{2,1,0:T(8,128)(2,1)}), bf16[8,512,128]{2,1,0:T(8,128)(2,1)S(1)}, u32[]{:S(2)}, u32[]{:S(2)}) %all-to-all-start.1) | async-done | bytes 1048608 | tf_op jit(solution)/shard_map/all_to_all | solution.py:44
  30.2 0.1 copy_bitcast_fusion
  30.3 5.4 %gather_fusion.2 = bf16[1024,1024]{1,0:T(8,128)(2,1)} fusion(bf16[512,1024]{1,0:T(8,128)(2,1)S(1)} %copy_bitcast_fusion, s32[1024]{0:T(1024)S(1)} %fusion.21), kind=kCustom, calls=%fused_computation.1.clone | custom fusion | bytes 4198400 | tf_op jit(solution)/shard_map/jit(_take)/gather | solution.py:30
  35.7 0.0 copy-start.1
  35.7 7.6 %all-gather.2.cloned.1.call-done = bf16[512,1024]{1,0:T(8,128)(2,1)} async-done(((bf16[512,128]{1,0:T(8,128)(2,1)}), bf16[512,1024]{1,0:T(8,128)(2,1)}) %all-gather.2.cloned.1.call-update) | async-done | bytes 1048592 | tf_op jit(solution)/shard_map/all_gather | solution.py:46
  43.3 7.4 %gather_fusion.1 = bf16[1024,1024]{1,0:T(8,128)(2,1)} fusion(bf16[512,1024]{1,0:T(8,128)(2,1)} %all-gather.2.cloned.1.call-done, s32[1024]{0:T(1024)S(1)} %fusion.21), kind=kCustom, calls=%fused_computation.clone | custom fusion | bytes 4198400 | tf_op jit(solution)/shard_map/jit(_take)/gather | solution.py:30
  50.7 0.0 copy-done.1
  50.7 2.0 broadcast_select_fusion.1
  52.7 1.7 broadcast_select_fusion.3
  54.4 66.2 %all_to_all.20 = bf16[64,16,1024]{2,1,0:T(8,128)(2,1)S(1)} all-to-all(bf16[64,16,1024]{2,1,0:T(8,128)(2,1)S(1)} %get-tuple-element.5), channel_id=1, replica_groups=mesh['ep'=64,'tp'=8] {'ep'}, dimensions={0} | all-to-all | bytes 4194304 | tf_op jit(solution)/shard_map/all_to_all | solution.py:51
  120.7 8.6 %all-to-all-start = ((bf16[64,16,1024]{2,1,0:T(8,128)(2,1)}), bf16[64,16,1024]{2,1,0:T(8,128)(2,1)}, u32[]{:S(2)}, u32[]{:S(2)}) async-start(bf16[64,16,1024]{2,1,0:T(8,128)(2,1)} %get-tuple-element.4), calls=%async_computation | async-start | bytes 4194304 | tf_op jit(solution)/shard_map/all_to_all | solution.py:52
  129.3 0.0 reduce-scatter.2.cloned.1.call-start
  129.3 0.0 copy-done
  129.3 2.6 fusion.11
  131.9 49.5 %all-to-all-done = bf16[64,16,1024]{2,1,0:T(8,128)(2,1)} async-done(((bf16[64,16,1024]{2,1,0:T(8,128)(2,1)}), bf16[64,16,1024]{2,1,0:T(8,128)(2,1)}, u32[]{:S(2)}, u32[]{:S(2)}) %all-to-all-start) | async-done | bytes 2097184 | tf_op jit(solution)/shard_map/all_to_all | solution.py:52
  181.5 4.9 %fusion.6 = bf16[1024,512]{1,0:T(8,128)(2,1)S(1)} fusion(f32[1024,512]{1,0:T(8,128)} %fusion.11, bf16[1024,1024]{1,0:T(8,128)(2,1)} %bitcast.4, bf16[1,512,1024]{2,1,0:T(8,128)(2,1)} %param.10), kind=kOutput, calls=%fused_computation.11 | convolution fusion | flops 1084227584 | bytes 6291456 | tf_op jit(solution)/shard_map/dot_general | solution.py:61
  186.4 0.0 copy-start.3
  186.4 1.0 copy-done.3
  187.4 3.2 %fusion.9 = f32[1024,1024]{1,0:T(8,128)} fusion(bf16[1024,512]{1,0:T(8,128)(2,1)S(1)} %fusion.6, bf16[1,1024,512]{2,1,0:T(8,128)(2,1)S(1)} %copy-done), kind=kOutput, calls=%fused_computation.22 | convolution fusion | flops 1073741824 | bytes 6291456 | tf_op jit(solution)/shard_map/dot_general | solution.py:71
  190.6 0.0 reduce-scatter.2.cloned.1.call-update
  190.6 0.1 convert_reduce_fusion
  190.7 0.1 select_reduce_fusion
  190.9 38.8 %reduce-scatter.2.cloned.1.call-done = f32[1024,128]{1,0:T(8,128)} async-done(((f32[1024,1024]{1,0:T(8,128)}), f32[1024,128]{1,0:T(8,128)}) %reduce-scatter.2.cloned.1.call-update) | async-done | bytes 524304 | tf_op jit(solution)/shard_map/reduce_scatter | solution.py:74
  229.7 1.8 convert_element_type.20
  231.4 13.4 %all-to-all-start.3 = ((bf16[64,16,128]{2,1,0:T(8,128)(2,1)}), bf16[64,16,128]{2,1,0:T(8,128)(2,1)S(1)}, u32[]{:S(2)}, u32[]{:S(2)}) async-start(bf16[64,16,128]{2,1,0:T(8,128)(2,1)} %bitcast.49), calls=%async_computation.4 | async-start | bytes 524288 | tf_op jit(solution)/shard_map/all_to_all | solution.py:76
  244.8 0.0 copy-start.4
  244.8 3.6 %fusion.7 = bf16[1,1024,512]{2,1,0:T(8,128)(2,1)} fusion(bf16[1024,1024]{1,0:T(8,128)(2,1)S(1)} %bitcast.48, bf16[1024,512]{1,0:T(8,128)(2,1)} %copy-done.3), kind=kOutput, calls=%fused_computation.19 | convolution fusion | flops 1074266112 | bytes 4194304 | tf_op jit(solution)/shard_map/dot_general | solution.py:68
  248.4 0.0 copy-done.4
  248.4 4.0 %fusion.8 = bf16[1,512,1024]{2,1,0:T(8,128)(2,1)} fusion(bf16[1024,1024]{1,0:T(8,128)(2,1)} %bitcast.4, f32[1024,512]{1,0:T(8,128)S(1)} %copy-done.4), kind=kOutput, calls=%fused_computation.20 | convolution fusion | flops 1078984704 | bytes 5242880 | tf_op jit(solution)/shard_map/dot_general | solution.py:65
  252.4 5.4 %all-to-all-done.3 = bf16[64,16,128]{2,1,0:T(8,128)(2,1)S(1)} async-done(((bf16[64,16,128]{2,1,0:T(8,128)(2,1)}), bf16[64,16,128]{2,1,0:T(8,128)(2,1)S(1)}, u32[]{:S(2)}, u32[]{:S(2)}) %all-to-all-start.3) | async-done | bytes 262176 | tf_op jit(solution)/shard_map/all_to_all | solution.py:76
  257.8 1.3 gather_fusion
  259.1 0.8 broadcast_select_fusion.4
  (8 shorter events, 0.1 us)
Async XLA Ops:
  7.2 122.1 %copy-start = (bf16[1,1024,512]{2,1,0:T(8,128)(2,1)S(1)}, bf16[1,1024,512]{2,1,0:T(8,128)(2,1)}, u32[]{:S(2)}) copy-start(bf16[1,1024,512]{2,1,0:T(8,128)(2,1)} %param.9) | copy-start | bytes 3145732
  7.2 7.1 %copy-start.2 = (s32[1,64]{1,0:T(1,128)S(1)}, s32[1,64]{1,0:T(1,128)}, u32[]{:S(2)}) copy-start(s32[1,64]{1,0:T(1,128)} %param.11) | copy-start | bytes 772
  7.2 36.1 %all-gather.2.cloned.1.call-start = ((), (), s32[]{:S(2)}) async-start(), calls=%async_computation.5 | async-start | bytes 1179648 | tf_op jit(solution)/shard_map/all_gather | solution.py:46
  9.9 20.2 %all-to-all-start.1 = ((bf16[8,512,128]{2,1,0:T(8,128)(2,1)}), bf16[8,512,128]{2,1,0:T(8,128)(2,1)S(1)}, u32[]{:S(2)}, u32[]{:S(2)}) async-start(bf16[8,512,128]{2,1,0:T(8,128)(2,1)} %stack.2), calls=%async_computation.1 | async-start | bytes 2097152 | tf_op jit(solution)/shard_map/all_to_all | solution.py:44
  35.7 15.0 %copy-start.1 = (bf16[1024,1024]{1,0:T(8,128)(2,1)S(1)}, bf16[1024,1024]{1,0:T(8,128)(2,1)}, u32[]{:S(2)}) copy-start(bf16[1024,1024]{1,0:T(8,128)(2,1)} %gather_fusion.2) | copy-start | bytes 6291460
  120.7 60.8 %all-to-all-start = ((bf16[64,16,1024]{2,1,0:T(8,128)(2,1)}), bf16[64,16,1024]{2,1,0:T(8,128)(2,1)}, u32[]{:S(2)}, u32[]{:S(2)}) async-start(bf16[64,16,1024]{2,1,0:T(8,128)(2,1)} %get-tuple-element.4), calls=%async_computation | async-start | bytes 4194304 | tf_op jit(solution)/shard_map/all_to_all | solution.py:52
  129.3 100.4 %reduce-scatter.2.cloned.1.call-start = ((), (), s32[]{:S(2)}) async-start(), calls=%async_computation.6 | async-start | bytes 4718592 | tf_op jit(solution)/shard_map/reduce_scatter | solution.py:74
  186.4 1.0 copy-start.3
  231.4 26.4 %all-to-all-start.3 = ((bf16[64,16,128]{2,1,0:T(8,128)(2,1)}), bf16[64,16,128]{2,1,0:T(8,128)(2,1)S(1)}, u32[]{:S(2)}, u32[]{:S(2)}) async-start(bf16[64,16,128]{2,1,0:T(8,128)(2,1)} %bitcast.49), calls=%async_computation.4 | async-start | bytes 524288 | tf_op jit(solution)/shard_map/all_to_all | solution.py:76
  244.8 3.6 %copy-start.4 = (f32[1024,512]{1,0:T(8,128)S(1)}, f32[1024,512]{1,0:T(8,128)}, u32[]{:S(2)}) copy-start(f32[1024,512]{1,0:T(8,128)} %fusion.11) | copy-start | bytes 6291460
Sparse Core Ops, SparseCore 0:
  10.1 33.1 all-gather.1
  190.7 38.8 reduce-scatter.1
